TPU v7x, 256 devices: a whole 4x4x8 slice. The times are simulated.
256 devices in a mesh: dp: 32 (over x, y, core), tensor: 8 (over z).
Axes of the slice: x: 4, y: 4, z: 8, core: 2. Of those that a mesh axis runs over, the one named last changes fastest.
Arguments:
- hidden: bfloat16 [32768, 8192], P(('dp', 'tensor')), may hold values from -50 to 50
- out_weight: bfloat16 [128256, 8192], P(('dp', 'tensor')), may hold values from -1 to 1
- loss_mask: int32 [32768], P(('dp', 'tensor')), may hold values from 0 to 1, as said below
- targets: int32 [32768], P(('dp', 'tensor')), may hold values from 0 to 128255
- kept_count: int32 [256], P(('dp', 'tensor')), may hold values from 0 to 1, as said below
Outputs:
- hidden_grad: bfloat16 [32768, 8192], P(('dp', 'tensor'))
- row_loss: float32 [32768], P(('dp', 'tensor'))
Inputs may be any that keep to these rules, and one draw needn't show every extreme that they name: `loss_mask`: each device's 128 rows hold at least 1 ones. `kept_count`: some entry equals 1 and some entry equals 0.
All inputs are finite; a program needn't handle non-finite values.
Results may differ from a plain program's by a relative error of at most 0.0026.
Values may be sent and summed in bfloat16 or wider, within the bound.
No kernel may reach another device: no remote copies, remote signals or barrier semaphores. Data moves between devices by JAX's collectives and lax.ppermute only.
A program may use at most 128 MiB of HBM per device.

v0:
```python
import jax
import jax.numpy as jnp
from jax import lax
from jax.sharding import PartitionSpec as P

CAP = 1
loss_scale = 128.0


def shards(hidden, out_weight, loss_mask, targets, kept_count):
    order_pos = jnp.cumsum(loss_mask) - 1
    kept_row = (loss_mask == 1) & (order_pos < kept_count[0])
    slot_ids = jnp.arange(CAP, dtype=jnp.int32)
    slot_hits = kept_row[None, :] & (order_pos[None, :] == slot_ids[:, None])
    packed = jnp.dot(
        slot_hits.astype(jnp.bfloat16), hidden, preferred_element_type=jnp.float32
    ).astype(jnp.bfloat16)
    slot_target = jnp.sum(jnp.where(slot_hits, targets[None, :], 0), axis=1)
    packed_target = jnp.where(jnp.any(slot_hits, axis=1), slot_target, -1)
    gathered, gathered_target = (
        lax.all_gather(packed, ("dp", "tensor"), axis=0, tiled=True),
        lax.all_gather(packed_target, ("dp", "tensor"), axis=0, tiled=True),
    )
    filled = gathered_target >= 0
    vocab_rows = out_weight.shape[0]
    device_pos = lax.axis_index(("dp", "tensor"))
    vocab_ids = device_pos * vocab_rows + jnp.arange(vocab_rows, dtype=jnp.int32)
    logits = jnp.einsum("rd,vd->rv", gathered, out_weight, preferred_element_type=jnp.float32)
    target_hit = vocab_ids[None, :] == gathered_target[:, None]
    local_top = jnp.max(logits, axis=1)
    local_pick = jnp.sum(jnp.where(target_hit, logits, 0.0), axis=1)
    row_top = lax.pmax(local_top, ("dp", "tensor"))
    shifted_total = jnp.sum(jnp.exp(logits - row_top[:, None]), axis=1)
    row_total, picked = lax.psum((shifted_total, local_pick), ("dp", "tensor"))
    log_total = row_top + jnp.log(row_total)
    slot_loss = jnp.where(filled, log_total - picked, 0.0)
    probabilities = jnp.exp(logits - log_total[:, None])
    coefficient = jnp.where(
        filled[:, None], probabilities - target_hit.astype(jnp.float32), 0.0
    ).astype(jnp.bfloat16)
    own_grad = lax.psum_scatter(
        jnp.dot(coefficient, out_weight, preferred_element_type=jnp.float32),
        ("dp", "tensor"),
        scatter_dimension=0,
        tiled=True,
    )
    own_grad = own_grad * loss_scale
    own_loss = lax.dynamic_slice_in_dim(slot_loss, device_pos * CAP, CAP, 0)
    slot_pos = jnp.clip(order_pos, 0, CAP - 1)
    hidden_grad = jnp.where(kept_row[:, None], own_grad[slot_pos], 0.0).astype(jnp.bfloat16)
    row_loss = jnp.where(kept_row, own_loss[slot_pos], 0.0)
    return (hidden_grad, row_loss)


def solution(mesh):
    in_specs = (
        P(("dp", "tensor"), None),
        P(("dp", "tensor"), None),
        P(("dp", "tensor")),
        P(("dp", "tensor")),
        P(("dp", "tensor")),
    )
    out_specs = (P(("dp", "tensor"), None), P(("dp", "tensor")))
    return jax.shard_map(shards, mesh=mesh, in_specs=in_specs, out_specs=out_specs, check_vma=False)
```

profile of v0, /device:TPU:97, one launch (start us, length us, event | category | flops | bytes accessed | tf_op | source)
XLA Modules:
  0.0 587.9 jit_solution(10313876143399885499)
XLA Ops:
  7.2 0.0 copy-start
  7.2 0.0 all-gather.3.cloned.1.call-start
  8.0 0.8 copy.9
  8.8 0.2 reduce-window.4
  8.9 0.1 compare_reduce_fusion
  9.1 1.3 select_reduce_fusion
  10.4 0.0 copy-done
  10.4 0.4 fusion.11
  10.8 0.6 convert_element_type.16
  11.4 0.0 all-gather.3.cloned.1.call-update
  11.4 0.0 all-reduce.5.cloned.1.call-start
  11.5 0.6 and_reduce_fusion
  13.4 0.1 dynamic-update-slice
  13.5 78.3 %all-reduce = s32[256]{0:T(256)S(1)} all-reduce(s32[256]{0:T(256)S(1)} %dynamic-update-slice), channel_id=1, replica_groups=mesh['dp'=32,'tensor'=8] {'dp','tensor'}, use_global_device_ids=true, to_apply=%add | all-reduce | flops 256 | bytes 2048
  91.8 37.0 %all-gather.3.cloned.1.call-done = bf16[2097152]{0:T(1024)(128)(2,1)} async-done(((bf16[8192]{0:T(1024)(128)(2,1)}), bf16[2097152]{0:T(1024)(128)(2,1)}) %all-gather.3.cloned.1.call-update) | async-done | bytes 4194320 | tf_op jit(solution)/shard_map/all_gather | solution.py:21
  128.8 7.3 %reshape.49 = bf16[256,8192]{1,0:T(8,128)(2,1)} reshape(bf16[2097152]{0:T(1024)(128)(2,1)} %all-gather.3.cloned.1.call-done) | data formatting | bytes 8388608 | tf_op jit(solution)/shard_map/all_gather | solution.py:21
  136.2 6.3 %fusion.15 = (f32[256]{0:T(256)S(1)}, f32[256,501]{0,1:T(8,128)S(1)}) fusion(bf16[256,8192]{1,0:T(8,128)(2,1)} %reshape.49, bf16[501,8192]{1,0:T(8,128)(2,1)} %param.6), kind=kOutput, calls=%fused_computation.29 | convolution fusion | flops 2101474304 | bytes 12916736 | tf_op jit(solution)/shard_map/rd,vd->rv/dot_general | solution.py:28
  142.4 74.6 %pmax.7 = f32[256]{0:T(256)S(1)} all-reduce(f32[256]{0:T(256)S(1)} %get-tuple-element.13), channel_id=1, replica_groups=mesh['dp'=32,'tensor'=8] {'dp','tensor'}, use_global_device_ids=true, to_apply=%region_4.5 | all-reduce | flops 256 | bytes 2048 | tf_op jit(solution)/shard_map/pmax | solution.py:32
  217.0 0.2 fusion.3
  217.2 73.7 %all-reduce.2 = (f32[256]{0:T(256)S(1)}, f32[256]{0:T(256)S(1)}) all-reduce(f32[256]{0:T(256)S(1)} %get-tuple-element.3, f32[256]{0:T(256)S(1)} %get-tuple-element.2), channel_id=1, replica_groups=mesh['dp'=32,'tensor'=8] {'dp','tensor'}, use_global_device_ids=true, to_apply=%region_6.7 | all-reduce | flops 512 | bytes 4096 | tf_op jit(solution)/shard_map/psum | solution.py:34
  290.9 9.1 %fusion.4 = f32[256,8192]{1,0:T(8,128)} fusion(bf16[501,8192]{1,0:T(8,128)(2,1)} %param.6, f32[256,501]{0,1:T(8,128)S(1)} %get-tuple-element.14, s32[256]{0:T(256)S(1)} %all-reduce, f32[256]{0:T(256)S(1)} %get-tuple-element.10, s32[501]{0:T(512)S(1)} %iota_add_fusion, pred[256]{0:T(512)(128)(4,1)S(1)} %get-tuple-element.9), kind=kOutput, calls=%fused_computation.8 | convolution fusion | flops 2102115840 | bytes 17114324 | tf_op jit(solution)/shard_map/dot_general | solution.py:42
  300.0 0.0 all-reduce.5.cloned.1.call-update
  300.1 0.6 dynamic_slice.5
  300.6 1.2 broadcast_select_fusion
  301.8 276.6 %all-reduce.5.cloned.1.call-done = f32[256,8192]{1,0:T(8,128)} async-done(((f32[256,8192]{1,0:T(8,128)}), f32[256,8192]{1,0:T(8,128)}) %all-reduce.5.cloned.1.call-update) | async-done | bytes 8388624
  578.4 1.0 dynamic-slice_multiply_fusion
  579.4 1.7 select_convert_fusion
  (3 shorter events, 0.0 us)
Async XLA Ops:
  7.2 3.2 copy-start
  7.2 121.7 %all-gather.3.cloned.1.call-start = ((), (), s32[]{:S(2)}) async-start(), calls=%async_computation | async-start | bytes 4210688 | tf_op jit(solution)/shard_map/all_gather | solution.py:21
  11.4 567.0 %all-reduce.5.cloned.1.call-start = ((), (), s32[]{:S(2)}) async-start(), calls=%async_computation.1 | async-start | bytes 16777216
Sparse Core Ops, SparseCore 0:
  12.3 116.5 all-gather.2
  300.2 278.2 all-reduce.4
where the time goes:
time: 589 us; the launch traced here: 588 us
  waiting for transfers between devices  314 us (53%)
  blocking collectives  227 us (39%)
  between operations  16.1 us (3%)
  matrix products  15.7 us (3%)
  local copies, waits for them, and re-layouts  8.79 us (1%)
  other arithmetic  6.82 us (1%)
    unnamed x3, waiting for transfers between devices  277 us
    unnamed x1, blocking collectives  78.3 us
    pmax x1, blocking collectives, shards(): row_top = lax.pmax(local_top, ('dp', 'tensor'))  74.6 us
    psum x1, blocking collectives, shards(): row_total, picked = lax.psum((shifted_total, local_pick), ('dp', 'tensor'))  73.7 us
    all_gather x1, waiting for transfers between devices, shards(): lax.all_gather(packed, ('dp', 'tensor'), axis=0, tiled=True)  37 us
  transfers between devices with their start and end apart: 2, of which 2 were waited for; matrix products, arithmetic and copies ran while one was open for 0% of the time, Pallas kernels for 0%

commit v1 on v0

--- a/solution.py
+++ b/solution.py
@@ -31,7 +31,7 @@
     local_pick = jnp.sum(jnp.where(target_hit, logits, 0.0), axis=1)
     row_top = lax.pmax(local_top, ("dp", "tensor"))
     shifted_total = jnp.sum(jnp.exp(logits - row_top[:, None]), axis=1)
-    row_total, picked = lax.psum((shifted_total, local_pick), ("dp", "tensor"))
+    row_total, picked = lax.psum(lax.psum((shifted_total, local_pick), "dp"), "tensor")
     log_total = row_top + jnp.log(row_total)
     slot_loss = jnp.where(filled, log_total - picked, 0.0)
     probabilities = jnp.exp(logits - log_total[:, None])

time: 589 us -> 592 us (level)
    psum x1 -> x2, blocking collectives: 73.7 us -> 74.7 us  [the longest x1 62.7 us: shards(): lax.psum((shifted_total, local_pick), 'dp')]
where the time goes in v1:
time: 592 us
  waiting for transfers between devices  316 us (53%)
  blocking collectives  228 us (39%)
  between operations  16.1 us (3%)
  matrix products  15.7 us (3%)
  local copies, waits for them, and re-layouts  8.79 us (1%)
  other arithmetic  6.83 us (1%)
    unnamed x3, waiting for transfers between devices  279 us
    unnamed x1, blocking collectives  78.3 us
    pmax x1, blocking collectives, shards(): row_top = lax.pmax(local_top, ('dp', 'tensor'))  74.6 us
    psum x1, blocking collectives, shards(): lax.psum((shifted_total, local_pick), 'dp')  62.7 us
    all_gather x1, waiting for transfers between devices, shards(): lax.all_gather(packed, ('dp', 'tensor'), axis=0, tiled=True)  37 us
    psum x1, blocking collectives, shards(): lax.psum(lax.psum((shifted_total, local_pick), 'dp'), 'tensor')  12 us
  transfers between devices with their start and end apart: 2, of which 2 were waited for; matrix products, arithmetic and copies ran while one was open for 0% of the time, Pallas kernels for 0%

profile of v1, /device:TPU:97, one launch (start us, length us, event | category | flops | bytes accessed | tf_op | source)
XLA Modules:
  0.0 591.7 jit_solution(13067195894622638861)
XLA Ops:
  7.2 0.0 copy-start
  7.2 0.0 all-gather.3.cloned.1.call-start
  8.0 0.8 copy.9
  8.8 0.2 reduce-window.4
  8.9 0.1 compare_reduce_fusion
  9.1 1.3 select_reduce_fusion
  10.4 0.0 copy-done
  10.4 0.4 fusion.11
  10.8 0.6 convert_element_type.16
  11.4 0.0 all-gather.3.cloned.1.call-update
  11.4 0.0 all-reduce.6.cloned.1.call-start
  11.5 0.6 and_reduce_fusion
  13.4 0.1 dynamic-update-slice
  13.5 78.3 %all-reduce = s32[256]{0:T(256)S(1)} all-reduce(s32[256]{0:T(256)S(1)} %dynamic-update-slice), channel_id=1, replica_groups=mesh['dp'=32,'tensor'=8] {'dp','tensor'}, use_global_device_ids=true, to_apply=%add | all-reduce | flops 256 | bytes 2048
  91.8 37.0 %all-gather.3.cloned.1.call-done = bf16[2097152]{0:T(1024)(128)(2,1)} async-done(((bf16[8192]{0:T(1024)(128)(2,1)}), bf16[2097152]{0:T(1024)(128)(2,1)}) %all-gather.3.cloned.1.call-update) | async-done | bytes 4194320 | tf_op jit(solution)/shard_map/all_gather | solution.py:21
  128.9 7.3 %reshape.49 = bf16[256,8192]{1,0:T(8,128)(2,1)} reshape(bf16[2097152]{0:T(1024)(128)(2,1)} %all-gather.3.cloned.1.call-done) | data formatting | bytes 8388608 | tf_op jit(solution)/shard_map/all_gather | solution.py:21
  136.2 6.3 %fusion.15 = (f32[256]{0:T(256)S(1)}, f32[256,501]{0,1:T(8,128)S(1)}) fusion(bf16[256,8192]{1,0:T(8,128)(2,1)} %reshape.49, bf16[501,8192]{1,0:T(8,128)(2,1)} %param.6), kind=kOutput, calls=%fused_computation.29 | convolution fusion | flops 2101474304 | bytes 12916736 | tf_op jit(solution)/shard_map/rd,vd->rv/dot_general | solution.py:28
  142.4 74.6 %pmax.7 = f32[256]{0:T(256)S(1)} all-reduce(f32[256]{0:T(256)S(1)} %get-tuple-element.15), channel_id=1, replica_groups=mesh['dp'=32,'tensor'=8] {'dp','tensor'}, use_global_device_ids=true, to_apply=%region_4.5 | all-reduce | flops 256 | bytes 2048 | tf_op jit(solution)/shard_map/pmax | solution.py:32
  217.0 0.2 fusion.3
  217.2 62.7 %all-reduce.2 = (f32[256]{0:T(256)S(1)}, f32[256]{0:T(256)S(1)}) all-reduce(f32[256]{0:T(256)S(1)} %get-tuple-element.3, f32[256]{0:T(256)S(1)} %get-tuple-element.2), channel_id=1, replica_groups=mesh['dp'=32,'tensor'=8] {'dp'}, use_global_device_ids=true, to_apply=%region_6.7 | all-reduce | flops 512 | bytes 4096 | tf_op jit(solution)/shard_map/psum | solution.py:34
  279.9 12.0 %all-reduce.3 = (f32[256]{0:T(256)S(1)}, f32[256]{0:T(256)S(1)}) all-reduce(f32[256]{0:T(256)S(1)} %get-tuple-element.6, f32[256]{0:T(256)S(1)} %get-tuple-element.7), channel_id=1, replica_groups=mesh['dp'=32,'tensor'=8] {'tensor'}, use_global_device_ids=true, to_apply=%region_7.8 | all-reduce | flops 512 | bytes 4096 | tf_op jit(solution)/shard_map/psum | solution.py:34
  291.9 9.1 %fusion.4 = f32[256,8192]{1,0:T(8,128)} fusion(bf16[501,8192]{1,0:T(8,128)(2,1)} %param.6, f32[256,501]{0,1:T(8,128)S(1)} %get-tuple-element.16, s32[256]{0:T(256)S(1)} %all-reduce, f32[256]{0:T(256)S(1)} %get-tuple-element.12, s32[501]{0:T(512)S(1)} %iota_add_fusion, pred[256]{0:T(512)(128)(4,1)S(1)} %get-tuple-element.11), kind=kOutput, calls=%fused_computation.8 | convolution fusion | flops 2102115840 | bytes 17114324 | tf_op jit(solution)/shard_map/dot_general | solution.py:42
  301.0 0.0 all-reduce.6.cloned.1.call-update
  301.0 0.6 dynamic_slice.5
  301.6 1.2 broadcast_select_fusion
  302.8 279.4 %all-reduce.6.cloned.1.call-done = f32[256,8192]{1,0:T(8,128)} async-done(((f32[256,8192]{1,0:T(8,128)}), f32[256,8192]{1,0:T(8,128)}) %all-reduce.6.cloned.1.call-update) | async-done | bytes 8388624
  582.2 1.0 dynamic-slice_multiply_fusion
  583.2 1.7 select_convert_fusion
  (3 shorter events, 0.0 us)
Async XLA Ops:
  7.2 3.2 copy-start
  7.2 121.7 %all-gather.3.cloned.1.call-start = ((), (), s32[]{:S(2)}) async-start(), calls=%async_computation | async-start | bytes 4210688 | tf_op jit(solution)/shard_map/all_gather | solution.py:21
  11.4 570.8 %all-reduce.6.cloned.1.call-start = ((), (), s32[]{:S(2)}) async-start(), calls=%async_computation.1 | async-start | bytes 16777216
Sparse Core Ops, SparseCore 0:
  12.3 116.5 all-gather.2
  301.2 281.0 all-reduce.5

commit v2 on v0

--- a/solution.py
+++ b/solution.py
@@ -18,7 +18,12 @@
     slot_target = jnp.sum(jnp.where(slot_hits, targets[None, :], 0), axis=1)
     packed_target = jnp.where(jnp.any(slot_hits, axis=1), slot_target, -1)
     gathered, gathered_target = (
-        lax.all_gather(packed, ("dp", "tensor"), axis=0, tiled=True),
+        jnp.concatenate(
+            lax.all_to_all(
+                jnp.stack([packed] * lax.axis_size(("dp", "tensor"))), ("dp", "tensor"), 0, 0
+            ),
+            axis=0,
+        ),
         lax.all_gather(packed_target, ("dp", "tensor"), axis=0, tiled=True),
     )
     filled = gathered_target >= 0

time: 589 us -> 686 us (1.16)
  blocking collectives: 227 us -> 281 us
  waiting for transfers between devices: 314 us -> 277 us
  local copies, waits for them, and re-layouts: 8.79 us -> 42 us
  other arithmetic: 6.82 us -> 33.1 us
  starting transfers between devices: 0.08 us -> 15.3 us
    unnamed x1, blocking collectives: 78.3 us -> 133 us
    all_gather x1 -> x0, waiting for transfers between devices: 37 us -> none  [shards(): lax.all_gather(packed, ('dp', 'tensor'), axis=0, tiled=True)]
    unnamed x4 -> x6, local copies, waits for them, and re-layouts: 0.13 us -> 34.5 us
    another operation x1 -> x2, other arithmetic: 0.17 us -> 27 us  [the longest x1 26.9 us: shards(): jnp.stack([packed] * lax.axis_size(('dp', 'tensor')))]
    all_to_all x0 -> x1, starting transfers between devices: none -> 15.3 us  [shards(): lax.all_to_all(jnp.stack([packed] * lax.axis_size(('dp', 'tensor'))), ('d...]
    all_gather x1 -> x0, local copies, waits for them, and re-layouts: 7.31 us -> none  [shards(): lax.all_gather(packed, ('dp', 'tensor'), axis=0, tiled=True)]
    unnamed x3 -> x2, waiting for transfers between devices: 277 us -> 277 us
  transfers between devices with their start and end apart: 2 -> 2, of which waited for: 2 -> 1; matrix products, arithmetic and copies ran while one was open for 0% -> 0% of each run, Pallas kernels for 0% -> 0%
where the time goes in v2:
time: 686 us; the launch traced here: 685 us
  blocking collectives  281 us (41%)
  waiting for transfers between devices  277 us (40%)
  local copies, waits for them, and re-layouts  42 us (6%)
  other arithmetic  33.1 us (5%)
  matrix products  20.9 us (3%)
  between operations  16.2 us (2%)
  starting transfers between devices  15.3 us (2%)
    unnamed x2, waiting for transfers between devices  277 us
    unnamed x1, blocking collectives  133 us
    psum x1, blocking collectives, shards(): row_total, picked = lax.psum((shifted_total, local_pick), ('dp', 'tensor'))  74.1 us
    pmax x1, blocking collectives, shards(): row_top = lax.pmax(local_top, ('dp', 'tensor'))  73.5 us
    unnamed x6, local copies, waits for them, and re-layouts  34.5 us
    another operation x1, other arithmetic, shards(): jnp.stack([packed] * lax.axis_size(('dp', 'tensor')))  26.9 us
    all_to_all x1, starting transfers between devices, shards(): lax.all_to_all(jnp.stack([packed] * lax.axis_size(('dp', 'tensor'))), ('d...  15.3 us
  transfers between devices with their start and end apart: 2, of which 1 were waited for; matrix products, arithmetic and copies ran while one was open for 0% of the time, Pallas kernels for 0%

profile of v2, /device:TPU:97, one launch (start us, length us, event | category | flops | bytes accessed | tf_op | source)
XLA Modules:
  0.0 684.7 jit_solution(1338794455101952133)
XLA Ops:
  7.2 0.0 copy-start
  8.0 0.8 copy.9
  8.7 0.2 reduce-window.4
  8.9 0.1 compare_reduce_fusion
  9.0 1.3 select_reduce_fusion
  10.3 0.0 copy-done
  10.3 0.4 fusion.14
  10.7 5.6 stack.2
  16.4 0.5 broadcast.62
  16.9 26.9 %reduce.8 = bf16[256,8192]{1,0:T(8,128)(2,1)} reduce(bf16[256,1,8192]{2,1,0:T(2,128)(2,1)} %stack.2, bf16[]{:T(256)} %broadcast.62), dimensions={1}, to_apply=%stack.2.reduce_sub_computation | reduce | bytes 8388610 | tf_op jit(solution)/shard_map/stack | solution.py:23
  43.7 7.8 %reshape.62 = bf16[256,2,4096]{2,1,0:T(2,128)(2,1)} reshape(bf16[256,8192]{1,0:T(8,128)(2,1)} %reduce.8) | data formatting | bytes 8388608
  51.5 15.3 %all-to-all-start = ((bf16[256,2,4096]{2,1,0:T(2,128)(2,1)}), bf16[256,2,4096]{2,1,0:T(2,128)(2,1)}, u32[]{:S(2)}, u32[]{:S(2)}) async-start(bf16[256,2,4096]{2,1,0:T(2,128)(2,1)} %reshape.62), calls=%async_computation | async-start | bytes 8388608 | tf_op jit(solution)/shard_map/all_to_all | solution.py:22
  66.8 0.0 all-reduce.5.cloned.1.call-start
  66.9 0.6 and_reduce_fusion
  68.9 0.1 dynamic-update-slice
  69.0 132.9 %all-reduce = s32[256]{0:T(256)S(1)} all-reduce(s32[256]{0:T(256)S(1)} %dynamic-update-slice), channel_id=1, replica_groups=mesh['dp'=32,'tensor'=8] {'dp','tensor'}, use_global_device_ids=true, to_apply=%add | all-reduce | flops 256 | bytes 2048
  201.9 0.0 all-to-all-done
  201.9 26.6 %reshape.63 = bf16[256,1,8192]{2,1,0:T(2,128)(2,1)} reshape(bf16[256,2,4096]{2,1,0:T(2,128)(2,1)} %all-to-all-done) | data formatting | bytes 8388608
  228.5 11.4 %fusion.18 = (f32[256]{0:T(256)S(1)}, f32[256,501]{0,1:T(8,128)S(1)}) fusion(bf16[501,8192]{1,0:T(8,128)(2,1)} %param.6, bf16[256,1,8192]{2,1,0:T(2,128)(2,1)} %reshape.63), kind=kOutput, calls=%fused_computation.32 | convolution fusion | flops 2101474304 | bytes 12916736 | tf_op jit(solution)/shard_map/rd,vd->rv/dot_general | solution.py:33
  239.9 73.5 %pmax.7 = f32[256]{0:T(256)S(1)} all-reduce(f32[256]{0:T(256)S(1)} %get-tuple-element.13), channel_id=1, replica_groups=mesh['dp'=32,'tensor'=8] {'dp','tensor'}, use_global_device_ids=true, to_apply=%region_4.5 | all-reduce | flops 256 | bytes 2048 | tf_op jit(solution)/shard_map/pmax | solution.py:37
  313.4 0.2 fusion.6
  313.5 74.1 %all-reduce.2 = (f32[256]{0:T(256)S(1)}, f32[256]{0:T(256)S(1)}) all-reduce(f32[256]{0:T(256)S(1)} %get-tuple-element.3, f32[256]{0:T(256)S(1)} %get-tuple-element.2), channel_id=1, replica_groups=mesh['dp'=32,'tensor'=8] {'dp','tensor'}, use_global_device_ids=true, to_apply=%region_6.7 | all-reduce | flops 512 | bytes 4096 | tf_op jit(solution)/shard_map/psum | solution.py:39
  387.6 9.1 %fusion.7 = f32[256,8192]{1,0:T(8,128)} fusion(bf16[501,8192]{1,0:T(8,128)(2,1)} %param.6, f32[256,501]{0,1:T(8,128)S(1)} %get-tuple-element.14, s32[256]{0:T(256)S(1)} %all-reduce, f32[256]{0:T(256)S(1)} %get-tuple-element.10, s32[501]{0:T(512)S(1)} %iota_add_fusion, pred[256]{0:T(512)(128)(4,1)S(1)} %get-tuple-element.9), kind=kOutput, calls=%fused_computation.11 | convolution fusion | flops 2102115840 | bytes 17114324 | tf_op jit(solution)/shard_map/dot_general | solution.py:47
  396.7 0.0 all-reduce.5.cloned.1.call-update
  396.8 0.6 dynamic_slice.5
  397.3 1.2 broadcast_select_fusion
  398.5 276.7 %all-reduce.5.cloned.1.call-done = f32[256,8192]{1,0:T(8,128)} async-done(((f32[256,8192]{1,0:T(8,128)}), f32[256,8192]{1,0:T(8,128)}) %all-reduce.5.cloned.1.call-update) | async-done | bytes 8388624
  675.2 1.0 dynamic-slice_multiply_fusion
  676.1 1.7 select_convert_fusion
  (4 shorter events, 0.0 us)
Async XLA Ops:
  7.2 3.2 copy-start
  51.5 150.4 %all-to-all-start = ((bf16[256,2,4096]{2,1,0:T(2,128)(2,1)}), bf16[256,2,4096]{2,1,0:T(2,128)(2,1)}, u32[]{:S(2)}, u32[]{:S(2)}) async-start(bf16[256,2,4096]{2,1,0:T(2,128)(2,1)} %reshape.62), calls=%async_computation | async-start | bytes 8388608 | tf_op jit(solution)/shard_map/all_to_all | solution.py:22
  66.8 608.3 %all-reduce.5.cloned.1.call-start = ((), (), s32[]{:S(2)}) async-start(), calls=%async_computation.1 | async-start | bytes 16777216
Sparse Core Ops, SparseCore 0:
  396.9 278.2 all-reduce.4
